TPU v7x, 32 devices: a whole 2x2x4 slice. The times are simulated.
32 devices in a mesh: row: 4 (over z), col: 8 (over y, x, core).
Axes of the slice: x: 2, y: 2, z: 4, core: 2. Of those that a mesh axis runs over, the one named last changes fastest.
Arguments:
- amplitudes: bfloat16 [16, 16, 12, 4096], P('row', 'col'), may hold values from -6 to 6
- integrals: bfloat16 [16, 16, 47, 4096], P('row', 'col'), may hold values from -0.1875 to 0.1875
- pair_lists: int32 [4, 12, 2], replicated, may hold values from 0 to 46, as said below
- tile_counts: int32 [4], replicated, may hold values from 1 to 12, as said below
Outputs:
- symmetric: float32 [16, 16, 12, 4096], P('row', 'col')
Inputs may be any that keep to these rules, and one draw needn't show every extreme that they name: `pair_lists`: each grid row lists 12 distinct ordered pairs of different tiles. `tile_counts`: the largest count equals 12.
All inputs are finite; a program needn't handle non-finite values.
Results may differ from a plain program's by a relative error of at most 0.0029.
Values may be sent and summed in bfloat16 or wider, within the bound.
No kernel may reach another device: no remote copies, remote signals or barrier semaphores. Data moves between devices by JAX's collectives and lax.ppermute only.
A program may use at most 128 MiB of HBM per device.

v0:
```python
import jax
import jax.numpy as jnp
from jax import lax
from jax.sharding import PartitionSpec as P

TILE = 64


def mirror_pairs(row_devices, col_devices, step):
    ratio = col_devices // row_devices
    pairs = []
    for row in range(row_devices):
        for col in range(col_devices):
            part = (col % ratio + step) % ratio
            pairs.append((row * col_devices + col, col // ratio * col_devices + row * ratio + part))
    return pairs


def on_device(amplitudes, integrals, pair_lists, tile_counts):
    occ_row, occ_col, slot_count, square = amplitudes.shape
    tile_width = TILE
    row_devices = lax.axis_size("row")
    col_devices = lax.axis_size("col")
    col_ratio = col_devices // row_devices
    my_row = lax.axis_index("row")
    my_col = lax.axis_index("col")
    partner_row = my_col // col_ratio
    tile_first = pair_lists[:, :, 0]
    tile_second = pair_lists[:, :, 1]
    packed = jnp.take(integrals, tile_second.reshape(-1), axis=2)
    packed = packed.reshape(occ_row, occ_col, row_devices, slot_count, square)
    received = lax.all_to_all(packed, "row", split_axis=2, concat_axis=0, tiled=True)
    received = received.reshape(occ_row * row_devices, occ_col, slot_count, square)
    piece = lax.all_gather(amplitudes, "col", axis=1, tiled=True)
    piece_count = piece.shape[1]
    left_tiles = piece.reshape(occ_row, piece_count, slot_count, tile_width, tile_width)
    right_tiles = received.reshape(piece_count, occ_col, slot_count, tile_width, tile_width)
    cycle_sum = jnp.einsum(
        "iksac,kjscb->ijsab", left_tiles, right_tiles, preferred_element_type=jnp.float32
    )
    my_count = lax.dynamic_index_in_dim(tile_counts, my_row, 0, keepdims=False)
    live_slots = (jnp.arange(slot_count, dtype=jnp.int32) < my_count).astype(jnp.float32)
    cycle_value = (cycle_sum * live_slots[None, None, :, None, None]).astype(jnp.bfloat16)
    cycle = cycle_value.reshape(occ_row, occ_col, slot_count, square)
    halves = cycle.reshape(col_ratio, occ_col, occ_col, slot_count, square)
    col_part = lax.rem(my_col, col_ratio)
    arrived = []
    for step in range(col_ratio):
        part = lax.rem(col_part + step, col_ratio)
        block = lax.dynamic_index_in_dim(halves, part, 0, keepdims=False)
        arrived.append(
            lax.ppermute(block, ("row", "col"), mirror_pairs(row_devices, col_devices, step))
        )
    arrived = jnp.stack(arrived)
    order = lax.rem(col_part - jnp.arange(col_ratio) + col_ratio, col_ratio)
    arrived = jnp.take(arrived, order, axis=0)
    mirror_block = jnp.moveaxis(arrived, 0, 1).reshape(occ_col, occ_row, slot_count, square)
    mirror_block = mirror_block.reshape(occ_col, occ_row, slot_count, tile_width, tile_width)
    mine_first = lax.dynamic_index_in_dim(tile_first, my_row, 0, keepdims=False)
    mine_second = lax.dynamic_index_in_dim(tile_second, my_row, 0, keepdims=False)
    their_first = lax.dynamic_index_in_dim(tile_first, partner_row, 0, keepdims=False)
    their_second = lax.dynamic_index_in_dim(tile_second, partner_row, 0, keepdims=False)
    pair_match = (
        (mine_first[:, None] == their_second[None, :])
        & (mine_second[:, None] == their_first[None, :])
    ).astype(jnp.bfloat16)
    crossed = jnp.einsum(
        "st,jitba->ijsab", pair_match, mirror_block, preferred_element_type=jnp.float32
    )
    own_part = cycle_value.astype(jnp.float32)
    symmetric = (own_part + crossed) * live_slots[None, None, :, None, None]
    return symmetric.reshape(occ_row, occ_col, slot_count, square)


def solution(mesh):
    return jax.shard_map(
        on_device,
        mesh=mesh,
        in_specs=(P("row", "col", None, None), P("row", "col", None, None), P(), P()),
        out_specs=P("row", "col", None, None),
        check_vma=False,
    )
```

profile of v0, /device:TPU:3, one launch (start us, length us, event | category | flops | bytes accessed | tf_op | source)
XLA Modules:
  0.0 234.9 jit_solution(8737630853103244513)
XLA Ops:
  6.5 2.8 %copy.23 = bf16[4,2,12,4096]{3,0,2,1:T(4,128)(2,1)} copy(bf16[4,2,12,4096]{3,1,2,0:T(2,128)(2,1)} %param.4) | data formatting | bytes 1572864 | tf_op args[0]
  9.3 0.8 fusion.33
  10.2 8.5 %gather_fusion = bf16[48,4,2,4096]{3,2,1,0:T(2,128)(2,1)} fusion(bf16[4,2,47,4096]{3,1,2,0:T(2,128)(2,1)S(1)} %copy-done, s32[1024]{0:T(1024)S(1)} %pad_clamp_fusion.1), kind=kCustom, calls=%fused_computation | custom fusion | bytes 6291648 | tf_op jit(solution)/shard_map/jit(_take)/gather | solution.py:30
  18.7 6.6 %broadcast_select_fusion = bf16[4,2,4,12,4096]{4,1,3,0,2:T(2,128)(2,1)} fusion(pred[4,12]{1,0:T(4,128)(4,1)S(1)} %compare_and_fusion.1, bf16[4,2,4,12,4096]{4,1,0,3,2:T(2,128)(2,1)} %bitcast.73), kind=kLoop, calls=%fused_computation.5 | loop fusion | flops 1572864 | bytes 6291504 | tf_op jit(solution)/shard_map/jit(_take)/select_n | solution.py:30
  25.4 5.0 %all-to-all-start = ((bf16[4,2,4,12,4096]{4,1,3,0,2:T(2,128)(2,1)}), bf16[4,2,4,12,4096]{4,1,3,0,2:T(2,128)(2,1)}, u32[]{:S(2)}, u32[]{:S(2)}) async-start(bf16[4,2,4,12,4096]{4,1,3,0,2:T(2,128)(2,1)} %broadcast_select_fusion), calls=%async_computation | async-start | bytes 6291456 | tf_op jit(solution)/shard_map/all_to_all | solution.py:32
  31.7 69.0 %all-to-all-done = bf16[4,2,4,12,4096]{4,1,3,0,2:T(2,128)(2,1)} async-done(((bf16[4,2,4,12,4096]{4,1,3,0,2:T(2,128)(2,1)}), bf16[4,2,4,12,4096]{4,1,3,0,2:T(2,128)(2,1)}, u32[]{:S(2)}, u32[]{:S(2)}) %all-to-all-start) | async-done | bytes 3145760 | tf_op jit(solution)/shard_map/all_to_all | solution.py:32
  100.6 11.1 %reshape_reshape.9 = bf16[16,2,12,64,64]{4,3,1,2,0:T(8,128)(2,1)} reshape(bf16[4,4,2,1,12,4096]{5,2,4,1,0,3:T(2,128)(2,1)} %bitcast.5) | data formatting | bytes 6291456 | tf_op jit(solution)/shard_map/reshape;reshape | solution.py:37
  111.7 9.3 %copy.24 = bf16[4,16,12,4096]{3,1,0,2:T(8,128)(2,1)} copy(bf16[4,16,12,4096]{3,0,2,1:T(4,128)(2,1)} %all-gather.2.cloned.1.call-done) | data formatting | bytes 12582912 | tf_op jit(solution)/shard_map/all_gather | solution.py:34
  121.1 17.9 %reshape.123 = bf16[4,16,12,64,64,1]{4,3,1,0,2,5:T(8,128)(2,1)} reshape(bf16[4,16,12,4096]{3,1,0,2:T(8,128)(2,1)} %copy.24) | data formatting | bytes 12582912 | tf_op jit(solution)/shard_map/reshape | solution.py:36
  139.0 11.1 %fusion.11 = bf16[4,2,12,64,64]{3,4,0,1,2:T(8,128)(2,1)S(1)} fusion(f32[12]{0:T(128)S(1)} %compare_convert_fusion, bf16[4,16,12,64,64,1]{4,3,1,0,2,5:T(8,128)(2,1)} %reshape.123, bf16[16,2,12,64,64]{4,3,1,2,0:T(8,128)(2,1)} %reshape_reshape.9), kind=kOutput, calls=%fused_computation.13 | convolution fusion | flops 806092800 | bytes 10223664 | tf_op jit(solution)/shard_map/iksac,kjscb->ijsab/dot_general | solution.py:38
  150.1 1.7 copy.26
  151.8 3.1 %reshape_reshape.10 = bf16[2,2,2,12,4096]{4,2,3,1,0:T(2,128)(2,1)S(1)} reshape(bf16[4,2,12,64,64]{4,3,1,2,0:T(8,128)(2,1)} %copy.26) | data formatting | bytes 1572864 | tf_op jit(solution)/shard_map/reshape;reshape | solution.py:45
  154.9 0.8 dynamic-slice_bitcast_fusion.1
  155.8 5.8 %collective-permute-start = (bf16[2,2,12,4096]{3,1,2,0:T(2,128)(2,1)S(1)}, bf16[2,2,12,4096]{3,1,2,0:T(2,128)(2,1)S(1)}, u32[]{:S(2)}, u32[]{:S(2)}) collective-permute-start(bf16[2,2,12,4096]{3,1,2,0:T(2,128)(2,1)S(1)} %get-tuple-element.5), channel_id=1, source_target_pairs={{0,0},{1,1},{2,8},{3,9},{4,16},{5,17},{6,24},{7,25},{8,2},{9,3},{1... | collective-permute-start | bytes 1179656 | tf_op jit(solution)/shard_map/ppermute | solution.py:52
  161.7 39.6 %collective-permute-done.1 = bf16[2,2,12,4096]{3,1,2,0:T(2,128)(2,1)S(1)} collective-permute-done((bf16[2,2,12,4096]{3,1,2,0:T(2,128)(2,1)S(1)}, bf16[2,2,12,4096]{3,1,2,0:T(2,128)(2,1)S(1)}, u32[]{:S(2)}, u32[]{:S(2)}) %collective-permute-start.1) | collective-permute-done | bytes 393248 | tf_op jit(solution)/shard_map/ppermute | solution.py:52
  201.3 8.9 %collective-permute-done = bf16[2,2,12,4096]{3,1,2,0:T(2,128)(2,1)S(1)} collective-permute-done((bf16[2,2,12,4096]{3,1,2,0:T(2,128)(2,1)S(1)}, bf16[2,2,12,4096]{3,1,2,0:T(2,128)(2,1)S(1)}, u32[]{:S(2)}, u32[]{:S(2)}) %collective-permute-start) | collective-permute-done | bytes 393248 | tf_op jit(solution)/shard_map/ppermute | solution.py:52
  210.2 1.1 pad_maximum_fusion
  211.4 2.1 gather_fusion.1
  214.2 0.8 copy.27
  215.0 1.0 reshape_reshape.11
  216.1 1.1 fusion.5
  217.5 2.7 %fusion.3 = f32[4,2,12,64,64]{3,4,0,1,2:T(8,128)} fusion(f32[2,4,64,64,12]{3,4,2,1,0:T(8,128)S(1)} %fusion.5, bf16[4,2,12,64,64]{3,4,0,1,2:T(8,128)(2,1)S(1)} %copy-done.3, f32[12]{0:T(128)S(1)} %compare_convert_fusion), kind=kLoop, calls=%fused_computation.7 | loop fusion | flops 1179648 | bytes 3932208 | tf_op jit(solution)/shard_map/mul | solution.py:71
  220.2 3.7 %copy.30 = f32[4,2,12,64,64]{4,3,1,2,0:T(8,128)} copy(f32[4,2,12,64,64]{3,4,0,1,2:T(8,128)} %fusion.3) | data formatting | bytes 3145728 | tf_op jit(solution)/shard_map/mul | solution.py:71
  223.9 4.2 %reshape.105 = f32[4,2,12,4096]{3,1,2,0:T(2,128)} reshape(f32[4,2,12,64,64]{4,3,1,2,0:T(8,128)} %copy.30) | data formatting | bytes 3145728 | tf_op jit(solution)/shard_map/reshape | solution.py:72
  (25 shorter events, 2.6 us)
Async XLA Ops:
  6.5 3.7 %copy-start = (bf16[4,2,47,4096]{3,1,2,0:T(2,128)(2,1)S(1)}, bf16[4,2,47,4096]{3,1,2,0:T(2,128)(2,1)}, u32[]{:S(2)}) copy-start(bf16[4,2,47,4096]{3,1,2,0:T(2,128)(2,1)} %param.5) | copy-start | bytes 9240580
  6.5 105.2 %all-gather.2.cloned.1.call-start = ((), (), s32[]{:S(2)}) async-start(), calls=%async_computation.1 | async-start | bytes 7077888 | tf_op jit(solution)/shard_map/all_gather | solution.py:34
  25.4 5.0 %copy-start.4 = (s32[4]{0:T(128)S(1)}, s32[4]{0:T(128)}, u32[]{:S(2)}) copy-start(s32[4]{0:T(128)} %param.7) | copy-start | bytes 52
  25.4 75.3 %all-to-all-start = ((bf16[4,2,4,12,4096]{4,1,3,0,2:T(2,128)(2,1)}), bf16[4,2,4,12,4096]{4,1,3,0,2:T(2,128)(2,1)}, u32[]{:S(2)}, u32[]{:S(2)}) async-start(bf16[4,2,4,12,4096]{4,1,3,0,2:T(2,128)(2,1)} %broadcast_select_fusion), calls=%async_computation | async-start | bytes 6291456 | tf_op jit(solution)/shard_map/all_to_all | solution.py:32
  150.1 5.6 %copy-start.2 = (bf16[4,2,12,64,64]{3,4,0,1,2:T(8,128)(2,1)}, bf16[4,2,12,64,64]{3,4,0,1,2:T(8,128)(2,1)S(1)}, u32[]{:S(2)}) copy-start(bf16[4,2,12,64,64]{3,4,0,1,2:T(8,128)(2,1)S(1)} %fusion.11) | copy-start | bytes 2359300
  155.7 45.6 %collective-permute-start.1 = (bf16[2,2,12,4096]{3,1,2,0:T(2,128)(2,1)S(1)}, bf16[2,2,12,4096]{3,1,2,0:T(2,128)(2,1)S(1)}, u32[]{:S(2)}, u32[]{:S(2)}) collective-permute-start(bf16[2,2,12,4096]{3,1,2,0:T(2,128)(2,1)S(1)} %get-tuple-element.6), channel_id=1, source_target_pairs={{0,1},{1,0},{2,9},{3,8},{4,17},{5,16},{6,25},{7,24},{8,3},{9,2},{1... | collective-permute-start | bytes 1179656 | tf_op jit(solution)/shard_map/ppermute | solution.py:52
  155.8 54.4 %collective-permute-start = (bf16[2,2,12,4096]{3,1,2,0:T(2,128)(2,1)S(1)}, bf16[2,2,12,4096]{3,1,2,0:T(2,128)(2,1)S(1)}, u32[]{:S(2)}, u32[]{:S(2)}) collective-permute-start(bf16[2,2,12,4096]{3,1,2,0:T(2,128)(2,1)S(1)} %get-tuple-element.5), channel_id=1, source_target_pairs={{0,0},{1,1},{2,8},{3,9},{4,16},{5,17},{6,24},{7,25},{8,2},{9,3},{1... | collective-permute-start | bytes 1179656 | tf_op jit(solution)/shard_map/ppermute | solution.py:52
  216.1 1.4 copy-start.3
  220.2 7.9 %copy-start.1 = (bf16[4,2,47,4096]{3,1,2,0:T(2,128)(2,1)S(1)}, bf16[4,2,47,4096]{3,1,2,0:T(2,128)(2,1)}, u32[]{:S(2)}) copy-start(bf16[4,2,47,4096]{3,1,2,0:T(2,128)(2,1)} %param.5) | copy-start | bytes 9240580
Sparse Core Ops, SparseCore 0:
  9.5 47.0 all-gather.1
where the time goes:
time: 236 us; the launch traced here: 235 us
  waiting for transfers between devices  118 us (50%)
  local copies, waits for them, and re-layouts  68.9 us (29%)
  between operations  13.6 us (6%)
  matrix products  12.2 us (5%)
  other arithmetic  11.9 us (5%)
  starting transfers between devices  10.9 us (5%)
    all_to_all x1, waiting for transfers between devices, on_device(): lax.all_to_all(packed, 'row', split_axis=2, concat_axis=0, tiled=True)  69 us
    ppermute x2, waiting for transfers between devices, on_device(): lax.ppermute(block, ('row', 'col'), mirror_pairs(row_devices, col_devices...  48.5 us
    reshape x1, local copies, waits for them, and re-layouts, on_device(): piece.reshape(occ_row, piece_count, slot_count, tile_width, tile_width)  17.9 us
    another operation x1, local copies, waits for them, and re-layouts, on_device(): received.reshape(piece_count, occ_col, slot_count, tile_width, tile_width)  11.1 us
    dot_general x1, matrix products, on_device(): jnp.einsum('iksac,kjscb->ijsab', left_tiles, right_tiles, preferred_eleme...  11.1 us
    all_gather x1, local copies, waits for them, and re-layouts, on_device(): piece = lax.all_gather(amplitudes, 'col', axis=1, tiled=True)  9.34 us
    gather x1, local copies, waits for them, and re-layouts, on_device(): packed = jnp.take(integrals, tile_second.reshape(-1), axis=2)  8.51 us
    select_n x2, other arithmetic, on_device(): packed = jnp.take(integrals, tile_second.reshape(-1), axis=2)  6.63 us
  transfers between devices with their start and end apart: 4, of which 3 were waited for; matrix products, arithmetic and copies ran while one was open for 12% of the time, Pallas kernels for 0%

commit v1 on v0

--- a/solution.py
+++ b/solution.py
@@ -4,6 +4,28 @@
 from jax.sharding import PartitionSpec as P
 
 TILE = 64
+
+
+def cut_along(array, dim, size):
+    before, after = (array.shape[:dim], array.shape[dim + 1 :])
+    return jnp.moveaxis(array.reshape(*before, size, -1, *after), dim, 0)
+
+
+def in_order(blocks, dim):
+    blocks = jnp.moveaxis(blocks, 0, dim)
+    shape = blocks.shape
+    return blocks.reshape(*shape[:dim], shape[dim] * shape[dim + 1], *shape[dim + 2 :])
+
+
+def exchange_directly(value, axis, split_dim, concat_dim):
+    size, mine = (lax.axis_size(axis), lax.axis_index(axis))
+    blocks = cut_along(value, split_dim, size)
+    done = [blocks[mine]]
+    for hop in range(1, size):
+        sent = blocks[(mine + hop) % size]
+        done.append(lax.ppermute(sent, axis, [(i, (i + hop) % size) for i in range(size)]))
+    blocks = jnp.stack(done)[(mine - jnp.arange(size)) % size]
+    return in_order(blocks, concat_dim)
 
 
 def mirror_pairs(row_devices, col_devices, step):
@@ -29,7 +51,7 @@
     tile_second = pair_lists[:, :, 1]
     packed = jnp.take(integrals, tile_second.reshape(-1), axis=2)
     packed = packed.reshape(occ_row, occ_col, row_devices, slot_count, square)
-    received = lax.all_to_all(packed, "row", split_axis=2, concat_axis=0, tiled=True)
+    received = exchange_directly(packed, "row", 2, 0)
     received = received.reshape(occ_row * row_devices, occ_col, slot_count, square)
     piece = lax.all_gather(amplitudes, "col", axis=1, tiled=True)
     piece_count = piece.shape[1]

time: 236 us -> 252 us (1.068)
  local copies, waits for them, and re-layouts: 68.9 us -> 85 us
  other arithmetic: 11.9 us -> 16.7 us
  waiting for transfers between devices: 118 us -> 114 us
    all_to_all x1 -> x0, waiting for transfers between devices: 69 us -> none  [on_device(): lax.all_to_all(packed, 'row', split_axis=2, concat_axis=0, tiled=True)]
    ppermute x0 -> x3, waiting for transfers between devices: none -> 65.3 us  [exchange_directly(): lax.ppermute(sent, axis, [(i, (i + hop) % size) for i in range(size)])]
    gather x0 -> x2, local copies, waits for them, and re-layouts: none -> 13.5 us  [exchange_directly(): blocks = jnp.stack(done)[(mine - jnp.arange(size)) % size]]
    another operation x0 -> x1, other arithmetic: none -> 5.08 us  [exchange_directly(): blocks = jnp.stack(done)[(mine - jnp.arange(size)) % size]]
    all_to_all x1 -> x0, starting transfers between devices: 4.97 us -> none  [on_device(): lax.all_to_all(packed, 'row', split_axis=2, concat_axis=0, tiled=True)]
    ppermute x0 -> x3, starting transfers between devices: none -> 3.79 us  [exchange_directly(): lax.ppermute(sent, axis, [(i, (i + hop) % size) for i in range(size)])]
    dynamic_slice x0 -> x1, local copies, waits for them, and re-layouts: none -> 2.58 us  [exchange_directly(): done = [blocks[mine]]]
  transfers between devices with their start and end apart: 4 -> 6, of which waited for: 3 -> 4; matrix products, arithmetic and copies ran while one was open for 12% -> 20% of each run, Pallas kernels for 0% -> 0%
where the time goes in v1:
time: 252 us; the launch traced here: 251 us
  waiting for transfers between devices  114 us (45%)
  local copies, waits for them, and re-layouts  85 us (34%)
  other arithmetic  16.7 us (7%)
  between operations  13.6 us (5%)
  matrix products  12.2 us (5%)
  starting transfers between devices  9.77 us (4%)
    ppermute x3, waiting for transfers between devices, exchange_directly(): lax.ppermute(sent, axis, [(i, (i + hop) % size) for i in range(size)])  65.3 us
    ppermute x2, waiting for transfers between devices, on_device(): lax.ppermute(block, ('row', 'col'), mirror_pairs(row_devices, col_devices...  48.5 us
    reshape x1, local copies, waits for them, and re-layouts, on_device(): piece.reshape(occ_row, piece_count, slot_count, tile_width, tile_width)  17.9 us
    gather x2, local copies, waits for them, and re-layouts, exchange_directly(): blocks = jnp.stack(done)[(mine - jnp.arange(size)) % size]  13.5 us
    another operation x1, local copies, waits for them, and re-layouts, on_device(): received.reshape(piece_count, occ_col, slot_count, tile_width, tile_width)  11.1 us
    dot_general x1, matrix products, on_device(): jnp.einsum('iksac,kjscb->ijsab', left_tiles, right_tiles, preferred_eleme...  11.1 us
    all_gather x1, local copies, waits for them, and re-layouts, on_device(): piece = lax.all_gather(amplitudes, 'col', axis=1, tiled=True)  9.35 us
    gather x1, local copies, waits for them, and re-layouts, on_device(): packed = jnp.take(integrals, tile_second.reshape(-1), axis=2)  8.51 us
  transfers between devices with their start and end apart: 6, of which 4 were waited for; matrix products, arithmetic and copies ran while one was open for 20% of the time, Pallas kernels for 0%

profile of v1, /device:TPU:3, one launch (start us, length us, event | category | flops | bytes accessed | tf_op | source)
XLA Modules:
  0.0 251.0 jit_solution(12822080569534361195)
XLA Ops:
  6.5 2.8 %copy.24 = bf16[4,2,12,4096]{3,0,2,1:T(4,128)(2,1)} copy(bf16[4,2,12,4096]{3,1,2,0:T(2,128)(2,1)} %param.4) | data formatting | bytes 1572864 | tf_op args[0]
  10.3 8.5 %gather_fusion = bf16[48,4,2,4096]{3,2,1,0:T(2,128)(2,1)} fusion(bf16[4,2,47,4096]{3,1,2,0:T(2,128)(2,1)S(1)} %copy-done, s32[1024]{0:T(1024)S(1)} %pad_clamp_fusion.2), kind=kCustom, calls=%fused_computation | custom fusion | bytes 6291648 | tf_op jit(solution)/shard_map/jit(_take)/gather | solution.py:52
  18.8 6.4 %copy_select_fusion = bf16[4,2,4,1,12,4096]{5,0,4,1,3,2:T(4,128)(2,1)S(1)} fusion(bf16[4,2,4,1,12,4096]{5,1,0,4,2,3:T(2,128)(2,1)} %bitcast.85, pred[4,12]{1,0:T(4,128)(4,1)S(1)} %compare_and_fusion.1), kind=kLoop, calls=%fused_computation.11 | loop fusion | flops 1572864 | bytes 6291504 | tf_op jit(solution)/shard_map/jit(_take)/select_n | solution.py:52
  25.2 2.6 %dynamic-slice_bitcast_fusion.3 = (bf16[1,4,2,1,12,4096]{5,1,4,2,0,3:T(4,128)(2,1)S(1)}, bf16[4,2,1,12,4096]{4,0,3,1,2:T(4,128)(2,1)}, bf16[4,2,1,12,4096]{4,0,3,1,2:T(4,128)(2,1)}, bf16[4,2,1,12,4096]{4,0,3,1,2:T(4,128)(2,1)}) fusion(bf16[4,2,4,1,12,4096]{5,0,4,1,3,2:T(4,128)(2,1)S(1)} %copy_select_fusion, s32[]{:T(128)S(6)} %select_n.125, ...), kind=kLoop, calls=%fused_computation.20 | loop fusion | bytes 6291472 | tf_op jit(solution)/shard_map/dynamic_slice | solution.py:23
  27.8 3.3 %collective-permute-start.2 = (bf16[4,2,1,12,4096]{4,0,3,1,2:T(4,128)(2,1)}, bf16[4,2,1,12,4096]{4,0,3,1,2:T(4,128)(2,1)S(1)}, u32[]{:S(2)}, u32[]{:S(2)}) collective-permute-start(bf16[4,2,1,12,4096]{4,0,3,1,2:T(4,128)(2,1)} %get-tuple-element.6), channel_id=1, source_target_pairs={{0,24},{8,0},{16,8},{24,16},{1,25},{9,1},{17,9},{25,17},{2,26},{10... | collective-permute-start | bytes 2359304 | tf_op jit(solution)/shard_map/ppermute | solution.py:26
  32.7 15.1 %collective-permute-done.2 = bf16[4,2,1,12,4096]{4,0,3,1,2:T(4,128)(2,1)S(1)} collective-permute-done((bf16[4,2,1,12,4096]{4,0,3,1,2:T(4,128)(2,1)}, bf16[4,2,1,12,4096]{4,0,3,1,2:T(4,128)(2,1)S(1)}, u32[]{:S(2)}, u32[]{:S(2)}) %collective-permute-start.2) | collective-permute-done | bytes 786464 | tf_op jit(solution)/shard_map/ppermute | solution.py:26
  47.9 50.2 %collective-permute-done.1 = bf16[4,2,1,12,4096]{4,0,3,1,2:T(4,128)(2,1)S(1)} collective-permute-done((bf16[4,2,1,12,4096]{4,0,3,1,2:T(4,128)(2,1)}, bf16[4,2,1,12,4096]{4,0,3,1,2:T(4,128)(2,1)S(1)}, u32[]{:S(2)}, u32[]{:S(2)}) %collective-permute-start.1) | collective-permute-done | bytes 786464 | tf_op jit(solution)/shard_map/ppermute | solution.py:26
  98.1 5.1 %maximum_bitcast_fusion = bf16[4,4,2,12,4096]{4,1,3,2,0:T(4,128)(2,1)} fusion(bf16[1,4,2,1,12,4096]{5,1,4,2,0,3:T(4,128)(2,1)S(1)} %bitcast.86, bf16[1,4,2,1,12,4096]{5,1,4,2,0,3:T(4,128)(2,1)S(1)} %bitcast.87, bf16[1,4,2,1,12,4096]{5,1,4,2,0,3:T(4,128)(2,1)} %bitcast.6, bf16[1,4,2,1,12,4096]{5,1,4,2,0,3:T(4,128)(2,1)S(1)} %get-tuple-element.5), kind=kLoop, calls=%fused_computation.6 | loop fusion | flops 4718592 | bytes 6291456 | tf_op jit(solution)/shard_map/stack | solution.py:27
  103.2 6.6 %gather_fusion.1 = bf16[4,4,2,12,4096]{4,1,3,2,0:T(4,128)(2,1)} fusion(bf16[4,4,2,12,4096]{4,1,3,2,0:T(4,128)(2,1)} %maximum_bitcast_fusion, s32[1024]{0:T(1024)S(1)} %pad_clamp_fusion.1), kind=kCustom, calls=%fused_computation.1 | custom fusion | bytes 6291472 | tf_op jit(solution)/shard_map/gather | solution.py:27
  109.8 6.9 %copy.23 = bf16[4,4,2,12,4096]{4,2,3,1,0:T(2,128)(2,1)} copy(bf16[4,4,2,12,4096]{4,1,3,2,0:T(4,128)(2,1)} %gather_fusion.1) | data formatting | bytes 6291456 | tf_op jit(solution)/shard_map/gather | solution.py:27
  116.7 11.1 %reshape_reshape_reshape.3 = bf16[16,2,12,64,64]{4,3,1,2,0:T(8,128)(2,1)} reshape(bf16[4,4,2,12,4096]{4,2,3,1,0:T(2,128)(2,1)} %copy.23) | data formatting | bytes 6291456 | tf_op jit(solution)/shard_map/reshape;reshape;reshape | solution.py:59
  127.8 9.4 %copy.25 = bf16[4,16,12,4096]{3,1,0,2:T(8,128)(2,1)} copy(bf16[4,16,12,4096]{3,0,2,1:T(4,128)(2,1)} %all-gather.2.cloned.1.call-done) | data formatting | bytes 12582912 | tf_op jit(solution)/shard_map/all_gather | solution.py:56
  137.1 17.9 %reshape.199 = bf16[4,16,12,64,64,1]{4,3,1,0,2,5:T(8,128)(2,1)} reshape(bf16[4,16,12,4096]{3,1,0,2:T(8,128)(2,1)} %copy.25) | data formatting | bytes 12582912 | tf_op jit(solution)/shard_map/reshape | solution.py:58
  155.0 11.1 %fusion.11 = bf16[4,2,12,64,64]{3,4,0,1,2:T(8,128)(2,1)S(1)} fusion(f32[12]{0:T(128)S(1)} %compare_convert_fusion, bf16[4,16,12,64,64,1]{4,3,1,0,2,5:T(8,128)(2,1)} %reshape.199, bf16[16,2,12,64,64]{4,3,1,2,0:T(8,128)(2,1)} %reshape_reshape_reshape.3), kind=kOutput, calls=%fused_computation.15 | convolution fusion | flops 806092800 | bytes 10223664 | tf_op jit(solution)/shard_map/iksac,kjscb->ijsab/dot_general | solution.py:60
  166.2 1.7 copy.27
  167.9 3.1 %reshape_reshape.7 = bf16[2,2,2,12,4096]{4,2,3,1,0:T(2,128)(2,1)S(1)} reshape(bf16[4,2,12,64,64]{4,3,1,2,0:T(8,128)(2,1)} %copy.27) | data formatting | bytes 1572864 | tf_op jit(solution)/shard_map/reshape;reshape | solution.py:67
  171.8 2.1 collective-permute-start.4
  173.9 3.8 %collective-permute-start.3 = (bf16[2,2,12,4096]{3,1,2,0:T(2,128)(2,1)S(1)}, bf16[2,2,12,4096]{3,1,2,0:T(2,128)(2,1)S(1)}, u32[]{:S(2)}, u32[]{:S(2)}) collective-permute-start(bf16[2,2,12,4096]{3,1,2,0:T(2,128)(2,1)S(1)} %get-tuple-element.9), channel_id=1, source_target_pairs={{0,0},{1,1},{2,8},{3,9},{4,16},{5,17},{6,24},{7,25},{8,2},{9,3},{1... | collective-permute-start | bytes 1179656 | tf_op jit(solution)/shard_map/ppermute | solution.py:74
  177.8 39.5 %collective-permute-done.4 = bf16[2,2,12,4096]{3,1,2,0:T(2,128)(2,1)S(1)} collective-permute-done((bf16[2,2,12,4096]{3,1,2,0:T(2,128)(2,1)S(1)}, bf16[2,2,12,4096]{3,1,2,0:T(2,128)(2,1)S(1)}, u32[]{:S(2)}, u32[]{:S(2)}) %collective-permute-start.4) | collective-permute-done | bytes 393248 | tf_op jit(solution)/shard_map/ppermute | solution.py:74
  217.4 8.9 %collective-permute-done.3 = bf16[2,2,12,4096]{3,1,2,0:T(2,128)(2,1)S(1)} collective-permute-done((bf16[2,2,12,4096]{3,1,2,0:T(2,128)(2,1)S(1)}, bf16[2,2,12,4096]{3,1,2,0:T(2,128)(2,1)S(1)}, u32[]{:S(2)}, u32[]{:S(2)}) %collective-permute-start.3) | collective-permute-done | bytes 393248 | tf_op jit(solution)/shard_map/ppermute | solution.py:74
  227.4 2.1 gather_fusion.2
  233.6 2.7 %fusion.3 = f32[4,2,12,64,64]{3,4,0,1,2:T(8,128)} fusion(f32[2,4,64,64,12]{3,4,2,1,0:T(8,128)S(1)} %fusion.5, bf16[4,2,12,64,64]{3,4,0,1,2:T(8,128)(2,1)S(1)} %copy-done.3, f32[12]{0:T(128)S(1)} %compare_convert_fusion), kind=kLoop, calls=%fused_computation.8 | loop fusion | flops 1179648 | bytes 3932208 | tf_op jit(solution)/shard_map/mul | solution.py:93
  236.3 3.7 %copy.31 = f32[4,2,12,64,64]{4,3,1,2,0:T(8,128)} copy(f32[4,2,12,64,64]{3,4,0,1,2:T(8,128)} %fusion.3) | data formatting | bytes 3145728 | tf_op jit(solution)/shard_map/mul | solution.py:93
  240.0 4.2 %reshape.170 = f32[4,2,12,4096]{3,1,2,0:T(2,128)} reshape(f32[4,2,12,64,64]{4,3,1,2,0:T(8,128)} %copy.31) | data formatting | bytes 3145728 | tf_op jit(solution)/shard_map/reshape | solution.py:94
  (35 shorter events, 8.5 us)
Async XLA Ops:
  6.5 3.7 %copy-start = (bf16[4,2,47,4096]{3,1,2,0:T(2,128)(2,1)S(1)}, bf16[4,2,47,4096]{3,1,2,0:T(2,128)(2,1)}, u32[]{:S(2)}) copy-start(bf16[4,2,47,4096]{3,1,2,0:T(2,128)(2,1)} %param.5) | copy-start | bytes 9240580
  6.5 121.2 %all-gather.2.cloned.1.call-start = ((), (), s32[]{:S(2)}) async-start(), calls=%async_computation | async-start | bytes 7077888 | tf_op jit(solution)/shard_map/all_gather | solution.py:56
  25.2 6.4 %copy-start.4 = (s32[4]{0:T(128)S(1)}, s32[4]{0:T(128)}, u32[]{:S(2)}) copy-start(s32[4]{0:T(128)} %param.7) | copy-start | bytes 52
  27.8 20.0 %collective-permute-start.2 = (bf16[4,2,1,12,4096]{4,0,3,1,2:T(4,128)(2,1)}, bf16[4,2,1,12,4096]{4,0,3,1,2:T(4,128)(2,1)S(1)}, u32[]{:S(2)}, u32[]{:S(2)}) collective-permute-start(bf16[4,2,1,12,4096]{4,0,3,1,2:T(4,128)(2,1)} %get-tuple-element.6), channel_id=1, source_target_pairs={{0,24},{8,0},{16,8},{24,16},{1,25},{9,1},{17,9},{25,17},{2,26},{10... | collective-permute-start | bytes 2359304 | tf_op jit(solution)/shard_map/ppermute | solution.py:26
  31.1 66.9 %collective-permute-start.1 = (bf16[4,2,1,12,4096]{4,0,3,1,2:T(4,128)(2,1)}, bf16[4,2,1,12,4096]{4,0,3,1,2:T(4,128)(2,1)S(1)}, u32[]{:S(2)}, u32[]{:S(2)}) collective-permute-start(bf16[4,2,1,12,4096]{4,0,3,1,2:T(4,128)(2,1)} %get-tuple-element.7), channel_id=1, source_target_pairs={{0,16},{8,24},{16,0},{24,8},{1,17},{9,25},{17,1},{25,9},{2,18},{10... | collective-permute-start | bytes 2359304 | tf_op jit(solution)/shard_map/ppermute | solution.py:26
  31.1 66.9 %collective-permute-start = (bf16[4,2,1,12,4096]{4,0,3,1,2:T(4,128)(2,1)}, bf16[4,2,1,12,4096]{4,0,3,1,2:T(4,128)(2,1)}, u32[]{:S(2)}, u32[]{:S(2)}) collective-permute-start(bf16[4,2,1,12,4096]{4,0,3,1,2:T(4,128)(2,1)} %get-tuple-element.8), channel_id=1, source_target_pairs={{0,8},{8,16},{16,24},{24,0},{1,9},{9,17},{17,25},{25,1},{2,10},{10... | collective-permute-start | bytes 2359304 | tf_op jit(solution)/shard_map/ppermute | solution.py:26
  166.1 5.6 %copy-start.2 = (bf16[4,2,12,64,64]{3,4,0,1,2:T(8,128)(2,1)}, bf16[4,2,12,64,64]{3,4,0,1,2:T(8,128)(2,1)S(1)}, u32[]{:S(2)}) copy-start(bf16[4,2,12,64,64]{3,4,0,1,2:T(8,128)(2,1)S(1)} %fusion.11) | copy-start | bytes 2359300
  171.8 45.6 %collective-permute-start.4 = (bf16[2,2,12,4096]{3,1,2,0:T(2,128)(2,1)S(1)}, bf16[2,2,12,4096]{3,1,2,0:T(2,128)(2,1)S(1)}, u32[]{:S(2)}, u32[]{:S(2)}) collective-permute-start(bf16[2,2,12,4096]{3,1,2,0:T(2,128)(2,1)S(1)} %get-tuple-element.10), channel_id=1, source_target_pairs={{0,1},{1,0},{2,9},{3,8},{4,17},{5,16},{6,25},{7,24},{8,3},{9,2},{1... | collective-permute-start | bytes 1179656 | tf_op jit(solution)/shard_map/ppermute | solution.py:74
  173.9 52.4 %collective-permute-start.3 = (bf16[2,2,12,4096]{3,1,2,0:T(2,128)(2,1)S(1)}, bf16[2,2,12,4096]{3,1,2,0:T(2,128)(2,1)S(1)}, u32[]{:S(2)}, u32[]{:S(2)}) collective-permute-start(bf16[2,2,12,4096]{3,1,2,0:T(2,128)(2,1)S(1)} %get-tuple-element.9), channel_id=1, source_target_pairs={{0,0},{1,1},{2,8},{3,9},{4,16},{5,17},{6,24},{7,25},{8,2},{9,3},{1... | collective-permute-start | bytes 1179656 | tf_op jit(solution)/shard_map/ppermute | solution.py:74
  232.1 1.4 copy-start.3
  236.2 7.9 %copy-start.1 = (bf16[4,2,47,4096]{3,1,2,0:T(2,128)(2,1)S(1)}, bf16[4,2,47,4096]{3,1,2,0:T(2,128)(2,1)}, u32[]{:S(2)}) copy-start(bf16[4,2,47,4096]{3,1,2,0:T(2,128)(2,1)} %param.5) | copy-start | bytes 9240580
Sparse Core Ops, SparseCore 0:
  9.5 47.0 all-gather.1
